TPU v7x, 32 devices: a whole 2x2x4 slice. The times are simulated.
32 devices in a mesh: dp: 8 (over z, x), ctx: 4 (over y, core).
Axes of the slice: x: 2, y: 2, z: 4, core: 2. Of those that a mesh axis runs over, the one named last changes fastest.
Arguments:
- block_input: bfloat16 [8, 512, 1024], P('dp', 'ctx'), may hold values from -6 to 6
- segment_ids: int32 [8, 512], P('dp'), may hold values from 0 to 2, never falling along the last dimension, each value on 1 to 320 neighbouring positions
- ln1_gain: bfloat16 [1024], P('dp'), may hold values from 0.25 to 1.75
- ln1_bias: bfloat16 [1024], P('dp'), may hold values from -3 to 3
- qkv_weight: bfloat16 [1024, 3, 1024], P('dp', None, 'ctx'), may hold values from -3 to 3
- query_bias: bfloat16 [1024], P('dp'), may hold values from -3 to 3
- value_bias: bfloat16 [1024], P('dp'), may hold values from -1.1953125 to 1.1953125
- proj_weight: bfloat16 [1024, 1024], P('ctx', 'dp'), may hold values from -0.75 to 0.75
- proj_bias: bfloat16 [1024], P('dp'), may hold values from -3 to 3
- ln2_gain: bfloat16 [1024], P('dp'), may hold values from 0.25 to 1.75
- ln2_bias: bfloat16 [1024], P('dp'), may hold values from -3 to 3
- fc_weight: bfloat16 [1024, 4096], P('dp', 'ctx'), may hold values from -0.1875 to 0.1875
- fc_bias: bfloat16 [4096], P('dp'), may hold values from -3 to 3
- out_weight: bfloat16 [4096, 1024], P('ctx', 'dp'), may hold values from -0.09375 to 0.09375
- out_bias: bfloat16 [1024], P('dp'), may hold values from -3 to 3
- cotangent: bfloat16 [8, 512, 1024], P('dp', 'ctx'), may hold values from -6 to 6
Outputs:
- block_output: bfloat16 [8, 512, 1024], P('dp', 'ctx')
- input_grad: float32 [8, 512, 1024], P('dp', 'ctx')
- ln1_gain_grad: float32 [1024], P('dp')
- ln1_bias_grad: float32 [1024], P('dp')
- qkv_weight_grad: float32 [1024, 3, 1024], P('dp', None, 'ctx')
- query_bias_grad: float32 [1024], P('dp')
- value_bias_grad: float32 [1024], P('dp')
- proj_weight_grad: float32 [1024, 1024], P('ctx', 'dp')
- proj_bias_grad: float32 [1024], P('dp')
- ln2_gain_grad: float32 [1024], P('dp')
- ln2_bias_grad: float32 [1024], P('dp')
- fc_weight_grad: float32 [1024, 4096], P('dp', 'ctx')
- fc_bias_grad: float32 [4096], P('dp')
- out_weight_grad: float32 [4096, 1024], P('ctx', 'dp')
- out_bias_grad: float32 [1024], P('dp')
Inputs may be any that keep to these rules, and one draw needn't show every extreme that they name: `segment_ids`: segment numbers never fall along a sequence.
All inputs are finite; a program needn't handle non-finite values.
Results may differ from a plain program's by a relative error of at most 0.019.
Values may be sent and summed in bfloat16 or wider, within the bound.
A program may use at most 128 MiB of HBM per device.

v0:
```python
import jax
import jax.numpy as jnp
from jax import lax
from jax.sharding import PartitionSpec as P

D = 1024
HD = 64
FF = 4096
NORM_EPS = 1e-05
GELU_ROOT = 0.7978845608028654
GELU_CUBE = 0.044715
MASK_VALUE = -1e30


def norm_forward(residual):
    row_mean = jnp.mean(residual, axis=-1, keepdims=True)
    centered = residual - row_mean
    row_var = jnp.mean(centered * centered, axis=-1, keepdims=True)
    inv_std = lax.rsqrt(row_var + NORM_EPS)
    return (centered * inv_std, inv_std)


def norm_backward(grad_in, normed, inv_std, gain):
    scaled = grad_in * gain
    mean_scaled = jnp.mean(scaled, axis=-1, keepdims=True)
    mean_cross = jnp.mean(scaled * normed, axis=-1, keepdims=True)
    return inv_std * (scaled - mean_scaled - normed * mean_cross)


def gelu_pair(pre_act):
    inner_arg = GELU_ROOT * (pre_act + GELU_CUBE * pre_act * pre_act * pre_act)
    tangent = jnp.tanh(inner_arg)
    activated = 0.5 * pre_act * (1.0 + tangent)
    gelu_slope = 0.5 * (1.0 + tangent) + 0.5 * pre_act * (1.0 - tangent * tangent) * GELU_ROOT * (
        1.0 + 3.0 * GELU_CUBE * pre_act * pre_act
    )
    return (activated, gelu_slope)


def masked_scores(query_heads, key_heads, allowed):
    raw_scores = jnp.einsum(
        "qhd,khd->hqk", query_heads, key_heads, preferred_element_type=jnp.float32
    ) * HD ** (-0.5)
    return jnp.where(allowed[None], raw_scores, MASK_VALUE)


def attend(query_heads, key_heads, value_heads, allowed):
    scores = masked_scores(query_heads, key_heads, allowed)
    top_score = jnp.max(scores, axis=-1, keepdims=True)
    log_total = top_score + jnp.log(jnp.sum(jnp.exp(scores - top_score), axis=-1, keepdims=True))
    attn_probs = jnp.where(allowed[None], jnp.exp(scores - log_total), 0.0)
    probs_half = attn_probs.astype(jnp.bfloat16)
    attended = jnp.einsum(
        "hqk,khd->qhd", probs_half, value_heads, preferred_element_type=jnp.float32
    )
    return (attended.reshape(query_heads.shape[0], -1).astype(jnp.bfloat16), log_total)


def attend_back(query_heads, key_heads, value_heads, allowed, log_total, grad_heads):
    scores = masked_scores(query_heads, key_heads, allowed)
    attn_probs = jnp.where(allowed[None], jnp.exp(scores - log_total), 0.0)
    probs_half = attn_probs.astype(jnp.bfloat16)
    prob_grad = jnp.einsum(
        "qhd,khd->hqk", grad_heads, value_heads, preferred_element_type=jnp.float32
    )
    value_part = jnp.einsum(
        "hqk,qhd->khd", probs_half, grad_heads, preferred_element_type=jnp.float32
    )
    delta_rows = jnp.sum(attn_probs * prob_grad, axis=-1, keepdims=True)
    score_grad = (attn_probs * (prob_grad - delta_rows) * HD ** (-0.5)).astype(jnp.bfloat16)
    query_grad = jnp.einsum(
        "hqk,khd->qhd", score_grad, key_heads, preferred_element_type=jnp.float32
    )
    key_part = jnp.einsum(
        "hqk,qhd->khd", score_grad, query_heads, preferred_element_type=jnp.float32
    )
    key_count = key_heads.shape[0]
    return (
        query_grad.reshape(query_heads.shape[0], -1),
        key_part.reshape(key_count, -1),
        value_part.reshape(key_count, -1),
    )


def place_part(part, whole_len, start):
    return lax.dynamic_update_slice_in_dim(jnp.zeros((whole_len,), jnp.float32), part, start, 0)


def body(
    block_input,
    segment_ids,
    ln1_gain,
    ln1_bias,
    qkv_weight,
    query_bias,
    value_bias,
    proj_weight,
    proj_bias,
    ln2_gain,
    ln2_bias,
    fc_weight,
    fc_bias,
    out_weight,
    out_bias,
    cotangent,
):
    tokens = block_input[0]
    seg_whole = segment_ids[0]
    grad_rows = cotangent[0]
    seq_length = seg_whole.shape[0]
    ctx_rank = lax.axis_index("ctx")
    key_pos = jnp.arange(seq_length, dtype=jnp.int32)
    resid_in = tokens.astype(jnp.float32)
    normed_one, inv_one = norm_forward(resid_in)
    grad_out = grad_rows.astype(jnp.float32)
    out_shift_grad = jnp.sum(grad_out, axis=0)
    vectors = lax.all_gather(
        jnp.concatenate(
            [
                ln1_gain,
                ln1_bias,
                query_bias,
                value_bias,
                proj_bias,
                ln2_gain,
                ln2_bias,
                out_bias,
                fc_bias,
            ]
        ),
        "dp",
        axis=0,
    )
    slice_len = ln1_gain.shape[0]
    dp_size = vectors.shape[0]
    ff_whole = fc_bias.shape[0] * dp_size

    def vector(at):
        return vectors[:, at * slice_len : (at + 1) * slice_len].astype(jnp.float32).reshape(-1)

    qkv_cols = lax.all_gather(qkv_weight, "dp", axis=0, tiled=True).reshape(D, -1)
    proj_rows = lax.all_gather(proj_weight, "dp", axis=1, tiled=True)
    fc_cols = lax.all_gather(fc_weight, "dp", axis=0, tiled=True)
    out_rows = lax.all_gather(out_weight, "dp", axis=1, tiled=True)
    quarter = proj_rows.shape[0]
    unit_part = fc_cols.shape[1]
    gain_first = vector(0)
    shift_first = vector(1)
    query_shift = lax.dynamic_slice_in_dim(vector(2), ctx_rank * quarter, quarter)
    value_shift = lax.dynamic_slice_in_dim(vector(3), ctx_rank * quarter, quarter)
    proj_shift = vector(4)
    gain_second = vector(5)
    shift_second = vector(6)
    out_shift = vector(7)
    fc_shift = lax.dynamic_slice_in_dim(
        vectors[:, 8 * slice_len :].astype(jnp.float32).reshape(-1), ctx_rank * unit_part, unit_part
    )
    local_heads = quarter // HD
    allowed = (key_pos[:, None] >= key_pos[None, :]) & (seg_whole[:, None] == seg_whole[None, :])
    hidden_one = (normed_one * gain_first + shift_first).astype(jnp.bfloat16)
    hidden_all, grad_all = (
        lax.all_gather(hidden_one, "ctx", axis=0, tiled=True),
        lax.all_gather(grad_rows, "ctx", axis=0, tiled=True),
    )
    qkv_out = jnp.dot(hidden_all, qkv_cols, preferred_element_type=jnp.float32)
    queries = (qkv_out[:, :quarter] + query_shift).astype(jnp.bfloat16)
    keys_here = qkv_out[:, quarter : 2 * quarter].astype(jnp.bfloat16)
    values_here = (qkv_out[:, 2 * quarter :] + value_shift).astype(jnp.bfloat16)
    query_heads = queries.reshape(seq_length, local_heads, HD)
    key_heads = keys_here.reshape(seq_length, local_heads, HD)
    value_heads = values_here.reshape(seq_length, local_heads, HD)
    attended, log_total = attend(query_heads, key_heads, value_heads, allowed)
    resid_mid = (
        resid_in
        + lax.psum_scatter(
            jnp.dot(attended, proj_rows, preferred_element_type=jnp.float32).astype(jnp.bfloat16),
            "ctx",
            scatter_dimension=0,
            tiled=True,
        ).astype(jnp.float32)
        + proj_shift
    )
    normed_two, inv_two = norm_forward(resid_mid)
    hidden_two = (normed_two * gain_second + shift_second).astype(jnp.bfloat16)
    hidden_two_all = lax.all_gather(hidden_two, "ctx", axis=0, tiled=True)
    pre_act = jnp.dot(hidden_two_all, fc_cols, preferred_element_type=jnp.float32) + fc_shift
    activated, gelu_slope = gelu_pair(pre_act)
    activated = activated.astype(jnp.bfloat16)
    block_output = (
        resid_mid
        + lax.psum_scatter(
            jnp.dot(activated, out_rows, preferred_element_type=jnp.float32).astype(jnp.bfloat16),
            "ctx",
            scatter_dimension=0,
            tiled=True,
        ).astype(jnp.float32)
        + out_shift
    ).astype(jnp.bfloat16)
    out_weight_grad = jnp.dot(activated.T, grad_all, preferred_element_type=jnp.float32)
    pre_grad = jnp.dot(grad_all, out_rows.T, preferred_element_type=jnp.float32) * gelu_slope
    fc_shift_grad = place_part(jnp.sum(pre_grad, axis=0), ff_whole, ctx_rank * unit_part)
    pre_grad_half = pre_grad.astype(jnp.bfloat16)
    fc_weight_grad = jnp.dot(hidden_two_all.T, pre_grad_half, preferred_element_type=jnp.float32)
    hidden_two_grad = lax.psum_scatter(
        jnp.dot(pre_grad_half, fc_cols.T, preferred_element_type=jnp.float32).astype(jnp.bfloat16),
        "ctx",
        scatter_dimension=0,
        tiled=True,
    ).astype(jnp.float32)
    gain_second_grad = jnp.sum(hidden_two_grad * normed_two, axis=0)
    shift_second_grad = jnp.sum(hidden_two_grad, axis=0)
    mid_grad = grad_out + norm_backward(hidden_two_grad, normed_two, inv_two, gain_second)
    proj_shift_grad = jnp.sum(mid_grad, axis=0)
    mid_grad_half = mid_grad.astype(jnp.bfloat16)
    mid_all = lax.all_gather(mid_grad_half, "ctx", axis=0, tiled=True)
    proj_weight_grad = jnp.dot(attended.T, mid_all, preferred_element_type=jnp.float32)
    attended_grad = jnp.dot(mid_all, proj_rows.T, preferred_element_type=jnp.float32).astype(
        jnp.bfloat16
    )
    grad_heads = attended_grad.reshape(seq_length, local_heads, HD)
    query_grad, key_grad, value_grad = attend_back(
        query_heads, key_heads, value_heads, allowed, log_total, grad_heads
    )
    query_shift_grad = place_part(jnp.sum(query_grad, axis=0), D, ctx_rank * quarter)
    value_shift_grad = place_part(jnp.sum(value_grad, axis=0), D, ctx_rank * quarter)
    qkv_grad = jnp.concatenate([query_grad, key_grad, value_grad], axis=1).astype(jnp.bfloat16)
    qkv_weight_grad = jnp.dot(hidden_all.T, qkv_grad, preferred_element_type=jnp.float32).reshape(
        D, 3, quarter
    )
    hidden_one_grad = lax.psum_scatter(
        jnp.dot(qkv_grad, qkv_cols.T, preferred_element_type=jnp.float32).astype(jnp.bfloat16),
        "ctx",
        scatter_dimension=0,
        tiled=True,
    ).astype(jnp.float32)
    gain_first_grad = jnp.sum(hidden_one_grad * normed_one, axis=0)
    shift_first_grad = jnp.sum(hidden_one_grad, axis=0)
    input_grad = mid_grad + norm_backward(hidden_one_grad, normed_one, inv_one, gain_first)
    half = jnp.bfloat16
    matrix_sums = (
        lax.psum_scatter(qkv_weight_grad.astype(half), "dp", scatter_dimension=0, tiled=True),
        lax.psum_scatter(proj_weight_grad.astype(half), "dp", scatter_dimension=1, tiled=True),
        lax.psum_scatter(fc_weight_grad.astype(half), "dp", scatter_dimension=0, tiled=True),
        lax.psum_scatter(out_weight_grad.astype(half), "dp", scatter_dimension=1, tiled=True),
    )
    matrix_sums = tuple((m.astype(jnp.float32) for m in matrix_sums))
    packed = jnp.concatenate(
        [
            v.reshape(dp_size, -1)
            for v in (
                gain_first_grad,
                shift_first_grad,
                query_shift_grad,
                value_shift_grad,
                proj_shift_grad,
                gain_second_grad,
                shift_second_grad,
                out_shift_grad,
                fc_shift_grad,
            )
        ],
        axis=1,
    )
    packed = lax.psum(packed, ("dp", "ctx"))
    mine = lax.dynamic_index_in_dim(packed, lax.axis_index("dp"), 0, keepdims=False)
    order = (0, 1, 2, 3, 4, 5, 6, 8, 7)
    pieces = [mine[i * slice_len : (i + 1) * slice_len] for i in range(8)] + [mine[8 * slice_len :]]
    vector_sums = tuple((pieces[i] for i in order))
    return (
        block_output[None],
        input_grad[None],
        vector_sums[0],
        vector_sums[1],
        matrix_sums[0],
        vector_sums[2],
        vector_sums[3],
        matrix_sums[1],
        vector_sums[4],
        vector_sums[5],
        vector_sums[6],
        matrix_sums[2],
        vector_sums[7],
        matrix_sums[3],
        vector_sums[8],
    )


def solution(mesh):
    return jax.shard_map(
        body,
        mesh=mesh,
        in_specs=(
            P("dp", "ctx", None),
            P("dp", None),
            P("dp"),
            P("dp"),
            P("dp", None, "ctx"),
            P("dp"),
            P("dp"),
            P("ctx", "dp"),
            P("dp"),
            P("dp"),
            P("dp"),
            P("dp", "ctx"),
            P("dp"),
            P("ctx", "dp"),
            P("dp"),
            P("dp", "ctx", None),
        ),
        out_specs=(
            P("dp", "ctx", None),
            P("dp", "ctx", None),
            P("dp"),
            P("dp"),
            P("dp", None, "ctx"),
            P("dp"),
            P("dp"),
            P("ctx", "dp"),
            P("dp"),
            P("dp"),
            P("dp"),
            P("dp", "ctx"),
            P("dp"),
            P("ctx", "dp"),
            P("dp"),
        ),
        check_vma=False,
    )
```

profile of v0, /device:TPU:0, one launch (start us, length us, event | category | flops | bytes accessed | tf_op | source)
XLA Modules:
  0.0 677.9 jit_solution(5925180839455593192)
XLA Ops:
  16.9 32.6 %all-gather.2 = bf16[8,1,1536]{2,1,0:T(2,128)(2,1)S(1)} all-gather(bf16[1,1,1536]{2,1,0:T(2,128)(2,1)S(1)} %reshape.258), channel_id=2, replica_groups=mesh['dp'=8,'ctx'=4] {'dp'}, dimensions={0}, use_global_device_ids=true | all-gather | bytes 27648 | tf_op jit(solution)/shard_map/all_gather | solution.py:117
  53.4 27.0 %all_gather.34 = bf16[256,1024]{1,0:T(8,128)(2,1)S(1)} all-gather(bf16[256,128]{1,0:T(8,128)(2,1)S(1)} %copy-done.4), channel_id=1, replica_groups=mesh['dp'=8,'ctx'=4] {'dp'}, dimensions={1}, use_global_device_ids=true | all-gather | bytes 589824 | tf_op jit(solution)/shard_map/all_gather | solution.py:142
  80.7 35.4 %all-gather.13.cloned.1.call-done = bf16[1024,3,256]{0,2,1:T(8,128)(2,1)} async-done(((bf16[128,3,256]{0,2,1:T(8,128)(2,1)}), bf16[1024,3,256]{0,2,1:T(8,128)(2,1)}) %all-gather.13.cloned.1.call-update) | async-done | bytes 1572880 | tf_op jit(solution)/shard_map/all_gather | solution.py:141
  125.8 22.5 %reduce-scatter.13.cloned.1.call-done = bf16[128,1024]{1,0:T(8,128)(2,1)} async-done(((bf16[512,1024]{1,0:T(8,128)(2,1)}), bf16[128,1024]{1,0:T(8,128)(2,1)}) %reduce-scatter.13.cloned.1.call-update) | async-done | bytes 262160 | tf_op jit(solution)/shard_map/reduce_scatter | solution.py:175
  154.1 45.4 %all-gather.17.cloned.1.call-done = bf16[1024,1024]{1,0:T(8,128)(2,1)} async-done(((bf16[128,1024]{1,0:T(8,128)(2,1)}), bf16[1024,1024]{1,0:T(8,128)(2,1)}) %all-gather.17.cloned.1.call-update) | async-done | bytes 2097168 | tf_op jit(solution)/shard_map/all_gather | solution.py:143
  199.4 17.2 %all-gather.15.cloned.1.call-done = bf16[512,1024]{1,0:T(8,128)(2,1)} async-done(((bf16[128,1024]{1,0:T(8,128)(2,1)}), bf16[512,1024]{1,0:T(8,128)(2,1)}) %all-gather.15.cloned.1.call-update) | async-done | bytes 1048592 | tf_op jit(solution)/shard_map/all_gather | solution.py:185
  216.7 4.5 fusion.85
  221.2 13.7 %all-gather.23.cloned.1.call-done = bf16[1,512,1024]{2,1,0:T(8,128)(2,1)} async-done(((bf16[1,128,1024]{2,1,0:T(8,128)(2,1)}), bf16[1,512,1024]{2,1,0:T(8,128)(2,1)}) %all-gather.23.cloned.1.call-update) | async-done | bytes 1048592 | tf_op jit(solution)/shard_map/all_gather | solution.py:163
  234.8 52.4 %all-gather.19.cloned.1.call-done = bf16[1024,1024]{1,0:T(8,128)(2,1)} async-done(((bf16[1024,128]{1,0:T(8,128)(2,1)}), bf16[1024,1024]{1,0:T(8,128)(2,1)}) %all-gather.19.cloned.1.call-update) | async-done | bytes 2097168 | tf_op jit(solution)/shard_map/all_gather | solution.py:144
  287.2 5.1 fusion.83
  294.8 4.8 convolution_convert_fusion.5
  299.6 18.2 %reduce-scatter.17.cloned.1.call-done = bf16[128,1024]{1,0:T(8,128)(2,1)} async-done(((bf16[512,1024]{1,0:T(8,128)(2,1)}), bf16[128,1024]{1,0:T(8,128)(2,1)}) %reduce-scatter.17.cloned.1.call-update) | async-done | bytes 262160 | tf_op jit(solution)/shard_map/reduce_scatter | solution.py:204
  319.1 26.0 %reduce-scatter.15.cloned.1.call-done = bf16[128,1024]{1,0:T(8,128)(2,1)} async-done(((bf16[512,1024]{1,0:T(8,128)(2,1)}), bf16[128,1024]{1,0:T(8,128)(2,1)}) %reduce-scatter.15.cloned.1.call-update) | async-done | bytes 262160 | tf_op jit(solution)/shard_map/reduce_scatter | solution.py:191
  348.0 4.8 convolution_convert_fusion
  352.9 4.0 copy.66
  357.0 4.2 convolution_convert_fusion.1
  372.2 7.7 %fusion.22 = bf16[4,64,512]{2,1,0:T(8,128)(2,1)S(1)} fusion(bf16[512,4,64]{0,2,1:T(8,128)(2,1)S(1)} %bitcast.205, f32[4,512,512]{1,2,0:T(8,128)} %fusion.86, f32[4,512,512]{1,2,0:T(8,128)} %copy-done.1, f32[4,512]{1,0:T(4,128)S(1)} %log_add_fusion, pred[512,512]{0,1:T(8,128)(4,1)S(1)} %fusion.29), kind=kOutput, calls=%fused_computation.31 | convolution fusion | flops 147982848 | bytes 9183232 | tf_op jit(solution)/shard_map/hqk,qhd->khd/dot_general | solution.py:74
  379.9 9.0 %fusion.80 = (f32[4,64]{1,0:T(4,128)S(1)}, bf16[512,4,64]{0,2,1:T(8,128)(2,1)S(1)}) fusion(bf16[512,4,64]{0,2,1:T(8,128)(2,1)S(1)} %bitcast.203, f32[4,512,512]{1,2,0:T(8,128)} %fusion.86, f32[4,512]{1,0:T(4,128)S(1)} %log_add_fusion, f32[4,512,512]{1,2,0:T(8,128)} %copy-done.1, pred[512,512]{0,1:T(8,128)(4,1)S(1)} %fusion.29), kind=kOutput, calls=%fused_computation.144 | convolution fusion | flops 148113664 | bytes 9184256 | tf_op jit(solution)/shard_map/hqk,khd->qhd/dot_general | solution.py:71
  399.9 37.2 %reduce-scatter.27.cloned.1.call-done = bf16[128,1024]{1,0:T(8,128)(2,1)} async-done(((bf16[1024,1024]{1,0:T(8,128)(2,1)}), bf16[128,1024]{1,0:T(8,128)(2,1)}) %reduce-scatter.27.cloned.1.call-update) | async-done | bytes 262160
  439.1 68.9 %reduce-scatter.23.cloned.1.call-done = bf16[128,1024]{1,0:T(8,128)(2,1)} async-done(((bf16[1024,1024]{1,0:T(8,128)(2,1)}), bf16[128,1024]{1,0:T(8,128)(2,1)}) %reduce-scatter.23.cloned.1.call-update) | async-done | bytes 262160 | tf_op jit(solution)/shard_map/reduce_scatter | solution.py:243
  509.8 63.9 %reduce-scatter.25.cloned.1.call-done = bf16[128,256]{1,0:T(8,128)(2,1)} async-done(((bf16[1024,256]{1,0:T(8,128)(2,1)}), bf16[128,256]{1,0:T(8,128)(2,1)}) %reduce-scatter.25.cloned.1.call-update) | async-done | bytes 65552
  575.3 24.6 %reduce-scatter.19.cloned.1.call-done = bf16[128,1024]{1,0:T(8,128)(2,1)} async-done(((bf16[512,1024]{1,0:T(8,128)(2,1)}), bf16[128,1024]{1,0:T(8,128)(2,1)}) %reduce-scatter.19.cloned.1.call-update) | async-done | bytes 262160 | tf_op jit(solution)/shard_map/reduce_scatter | solution.py:230
  601.2 40.2 %psum.7 = f32[8,1536]{1,0:T(8,128)S(1)} all-reduce(f32[8,1536]{1,0:T(8,128)S(1)} %constant_dynamic-update-slice_fusion), channel_id=1, replica_groups=mesh['dp'=8,'ctx'=4] {'dp','ctx'}, use_global_device_ids=true, to_apply=%region_24.25 | all-reduce | flops 12288 | bytes 98304 | tf_op jit(solution)/shard_map/psum | solution.py:264
  644.7 25.0 %reduce-scatter.21.cloned.1.call-done = bf16[128,3,256]{2,0,1:T(8,128)(2,1)} async-done(((bf16[1024,3,256]{2,0,1:T(8,128)(2,1)}), bf16[128,3,256]{2,0,1:T(8,128)(2,1)}) %reduce-scatter.21.cloned.1.call-update) | async-done | bytes 196624 | tf_op jit(solution)/shard_map/reduce_scatter | solution.py:241
  (139 shorter events, 69.2 us)
Async XLA Ops:
  7.2 46.3 %copy-start.4 = (bf16[256,128]{1,0:T(8,128)(2,1)S(1)}, bf16[256,128]{1,0:T(8,128)(2,1)}, u32[]{:S(2)}) copy-start(bf16[256,128]{1,0:T(8,128)(2,1)} %param.23) | copy-start | bytes 196612
  7.2 73.3 %copy-start.5 = (s32[1,512]{1,0:T(1,128)S(1)}, s32[1,512]{1,0:T(1,128)}, u32[]{:S(2)}) copy-start(s32[1,512]{1,0:T(1,128)} %param.17) | copy-start | bytes 6148
  7.2 73.5 %all-gather.11.cloned.1.call-start = ((), (), s32[]{:S(2)}) async-start(), calls=%async_computation.8 | async-start | bytes 1310720 | tf_op jit(solution)/shard_map/all_gather | solution.py:162
  51.4 64.8 %all-gather.13.cloned.1.call-start = ((), (), s32[]{:S(2)}) async-start(), calls=%async_computation.9 | async-start | bytes 1769472 | tf_op jit(solution)/shard_map/all_gather | solution.py:141
  53.2 95.1 %reduce-scatter.13.cloned.1.call-start = ((), (), s32[]{:S(2)}) async-start(), calls=%async_computation.10 | async-start | bytes 1310720 | tf_op jit(solution)/shard_map/reduce_scatter | solution.py:175
  123.7 24.6 %copy-start = (bf16[1,128,1024]{2,1,0:T(8,128)(2,1)S(1)}, bf16[1,128,1024]{2,1,0:T(8,128)(2,1)}, u32[]{:S(2)}) copy-start(bf16[1,128,1024]{2,1,0:T(8,128)(2,1)} %param.16) | copy-start | bytes 786436
  125.2 74.2 %all-gather.17.cloned.1.call-start = ((), (), s32[]{:S(2)}) async-start(), calls=%async_computation.12 | async-start | bytes 2359296 | tf_op jit(solution)/shard_map/all_gather | solution.py:143
  125.8 90.9 %all-gather.15.cloned.1.call-start = ((), (), s32[]{:S(2)}) async-start(), calls=%async_computation.11 | async-start | bytes 1310720 | tf_op jit(solution)/shard_map/all_gather | solution.py:185
  152.5 82.4 %all-gather.23.cloned.1.call-start = ((), (), s32[]{:S(2)}) async-start(), calls=%async_computation.20 | async-start | bytes 1310720 | tf_op jit(solution)/shard_map/all_gather | solution.py:163
  153.0 134.2 %all-gather.19.cloned.1.call-start = ((), (), s32[]{:S(2)}) async-start(), calls=%async_computation.13 | async-start | bytes 2359296 | tf_op jit(solution)/shard_map/all_gather | solution.py:144
  153.8 164.0 %reduce-scatter.17.cloned.1.call-start = ((), (), s32[]{:S(2)}) async-start(), calls=%async_computation.15 | async-start | bytes 1310720 | tf_op jit(solution)/shard_map/reduce_scatter | solution.py:204
  287.2 5.1 copy-start.6
  292.3 2.4 copy-start.10
  294.7 23.1 %copy-start.2 = (bf16[128,1024]{1,0:T(8,128)(2,1)S(1)}, bf16[128,1024]{1,0:T(8,128)(2,1)}, u32[]{:S(2)}) copy-start(bf16[128,1024]{1,0:T(8,128)(2,1)} %reduce-scatter.13.cloned.1.call-done) | copy-start | bytes 786436
  294.7 50.5 %copy-start.3 = (bf16[1,128,1024]{2,1,0:T(8,128)(2,1)S(1)}, bf16[1,128,1024]{2,1,0:T(8,128)(2,1)}, u32[]{:S(2)}) copy-start(bf16[1,128,1024]{2,1,0:T(8,128)(2,1)} %param.31) | copy-start | bytes 786436
  294.7 50.5 %reduce-scatter.15.cloned.1.call-start = ((), (), s32[]{:S(2)}) async-start(), calls=%async_computation.14 | async-start | bytes 1310720 | tf_op jit(solution)/shard_map/reduce_scatter | solution.py:191
  299.6 65.3 %all-gather.21.cloned.1.call-start = ((), (), s32[]{:S(2)}) async-start(), calls=%async_computation.16 | async-start | bytes 1310720 | tf_op jit(solution)/shard_map/all_gather | solution.py:215
  348.0 89.1 %reduce-scatter.27.cloned.1.call-start = ((), (), s32[]{:S(2)}) async-start(), calls=%async_computation.22 | async-start | bytes 2359296
  356.9 151.1 %reduce-scatter.23.cloned.1.call-start = ((), (), s32[]{:S(2)}) async-start(), calls=%async_computation.19 | async-start | bytes 2359296 | tf_op jit(solution)/shard_map/reduce_scatter | solution.py:243
  361.2 212.5 %reduce-scatter.25.cloned.1.call-start = ((), (), s32[]{:S(2)}) async-start(), calls=%async_computation.21 | async-start | bytes 589824
  371.9 227.9 %reduce-scatter.19.cloned.1.call-start = ((), (), s32[]{:S(2)}) async-start(), calls=%async_computation.17 | async-start | bytes 1310720 | tf_op jit(solution)/shard_map/reduce_scatter | solution.py:230
  388.9 3.9 copy-start.8
  389.0 3.9 copy-start.7
  394.9 274.7 %reduce-scatter.21.cloned.1.call-start = ((), (), s32[]{:S(2)}) async-start(), calls=%async_computation.18 | async-start | bytes 1769472 | tf_op jit(solution)/shard_map/reduce_scatter | solution.py:241
  (2 other events, 4.0 us)
Sparse Core Ops, SparseCore 0:
  51.5 17.5 all-gather.10
  71.7 44.3 all-gather.12
  125.3 22.9 reduce-scatter.12
  150.3 49.0 all-gather.16
  201.4 15.2 all-gather.14
  218.1 16.6 all-gather.22
  236.9 50.3 all-gather.18
  294.8 22.9 reduce-scatter.16
  320.4 24.7 reduce-scatter.14
  348.1 16.6 all-gather.20
  368.4 68.6 reduce-scatter.26
  440.5 67.4 reduce-scatter.22
  511.9 61.6 reduce-scatter.24
  576.0 23.7 reduce-scatter.18
  603.1 66.4 reduce-scatter.20
where the time goes:
time: 679 us; the launch traced here: 678 us
  waiting for transfers between devices  456 us (67%)
  blocking collectives  99.8 us (15%)
  matrix products  63.1 us (9%)
  other arithmetic  21.9 us (3%)
  local copies, waits for them, and re-layouts  21.7 us (3%)
  between operations  14.3 us (2%)
    unnamed x17, waiting for transfers between devices  103 us
    reduce_scatter x1, waiting for transfers between devices, body(): lax.psum_scatter(fc_weight_grad.astype(half), 'dp', scatter_dimension=0,...  68.9 us
    all_gather x1, waiting for transfers between devices, body(): out_rows = lax.all_gather(out_weight, 'dp', axis=1, tiled=True)  52.4 us
    all_gather x1, waiting for transfers between devices, body(): fc_cols = lax.all_gather(fc_weight, 'dp', axis=0, tiled=True)  45.4 us
    psum x1, blocking collectives, body(): packed = lax.psum(packed, ('dp', 'ctx'))  40.2 us
    all_gather x1, waiting for transfers between devices, body(): lax.all_gather(qkv_weight, 'dp', axis=0, tiled=True).reshape(D, -1)  35.4 us
    all_gather x1, blocking collectives, body(): lax.all_gather(jnp.concatenate([ln1_gain, ln1_bias, query_bias, value_bia...  32.6 us
    all_gather x1, blocking collectives, body(): proj_rows = lax.all_gather(proj_weight, 'dp', axis=1, tiled=True)  27 us
  transfers between devices with their start and end apart: 15, of which 14 were waited for; matrix products, arithmetic and copies ran while one was open for 11% of the time, Pallas kernels for 0%

commit v1 on v0

--- a/solution.py
+++ b/solution.py
@@ -261,7 +261,8 @@
         ],
         axis=1,
     )
-    packed = lax.psum(packed, ("dp", "ctx"))
+    blocks = lax.all_gather(packed, ("dp", "ctx"), axis=0, tiled=False)
+    packed = blocks.sum(axis=0)
     mine = lax.dynamic_index_in_dim(packed, lax.axis_index("dp"), 0, keepdims=False)
     order = (0, 1, 2, 3, 4, 5, 6, 8, 7)
     pieces = [mine[i * slice_len : (i + 1) * slice_len] for i in range(8)] + [mine[8 * slice_len :]]

time: 679 us -> 763 us (1.12)
  waiting for transfers between devices: 456 us -> 576 us
  blocking collectives: 99.8 us -> 59.6 us
    all_gather x0 -> x1, waiting for transfers between devices: none -> 54.9 us  [body(): blocks = lax.all_gather(packed, ('dp', 'ctx'), axis=0, tiled=False)]
    reduce_scatter x1, waiting for transfers between devices: 25 us -> 65.7 us  [body(): lax.psum_scatter(qkv_weight_grad.astype(half), 'dp', scatter_dimension=0,...]
    psum x1 -> x0, blocking collectives: 40.2 us -> none  [body(): packed = lax.psum(packed, ('dp', 'ctx'))]
    unnamed x17 -> x18, waiting for transfers between devices: 103 us -> 136 us
    reduce_scatter x1, waiting for transfers between devices: 24.6 us -> 2.95 us  [body(): lax.psum_scatter(jnp.dot(qkv_grad, qkv_cols.T, preferred_element_type=jnp...]
    all_gather x1, waiting for transfers between devices: 3.64 us -> 16.6 us  [body(): mid_all = lax.all_gather(mid_grad_half, 'ctx', axis=0, tiled=True)]
    unnamed x46 -> x54, local copies, waits for them, and re-layouts: 16.7 us -> 20.5 us
  transfers between devices with their start and end apart: 15 -> 16, of which waited for: 14 -> 15; matrix products, arithmetic and copies ran while one was open for 11% -> 6% of each run, Pallas kernels for 0% -> 0%
where the time goes in v1:
time: 763 us; the launch traced here: 762 us
  waiting for transfers between devices  576 us (75%)
  matrix products  62.7 us (8%)
  blocking collectives  59.6 us (8%)
  local copies, waits for them, and re-layouts  25.5 us (3%)
  other arithmetic  22.5 us (3%)
  between operations  14.3 us (2%)
    unnamed x18, waiting for transfers between devices  136 us
    reduce_scatter x1, waiting for transfers between devices, body(): lax.psum_scatter(fc_weight_grad.astype(half), 'dp', scatter_dimension=0,...  69 us
    reduce_scatter x1, waiting for transfers between devices, body(): lax.psum_scatter(qkv_weight_grad.astype(half), 'dp', scatter_dimension=0,...  65.7 us
    all_gather x1, waiting for transfers between devices, body(): blocks = lax.all_gather(packed, ('dp', 'ctx'), axis=0, tiled=False)  54.9 us
    all_gather x1, waiting for transfers between devices, body(): out_rows = lax.all_gather(out_weight, 'dp', axis=1, tiled=True)  52.4 us
    all_gather x1, waiting for transfers between devices, body(): fc_cols = lax.all_gather(fc_weight, 'dp', axis=0, tiled=True)  45.4 us
    all_gather x1, waiting for transfers between devices, body(): lax.all_gather(qkv_weight, 'dp', axis=0, tiled=True).reshape(D, -1)  35.4 us
    all_gather x1, blocking collectives, body(): lax.all_gather(jnp.concatenate([ln1_gain, ln1_bias, query_bias, value_bia...  32.6 us
  transfers between devices with their start and end apart: 16, of which 15 were waited for; matrix products, arithmetic and copies ran while one was open for 6% of the time, Pallas kernels for 0%

profile of v1, /device:TPU:0, one launch (start us, length us, event | category | flops | bytes accessed | tf_op | source)
XLA Modules:
  0.0 761.7 jit_solution(7486782388946372886)
XLA Ops:
  16.9 32.6 %all-gather.3 = bf16[8,1,1536]{2,1,0:T(2,128)(2,1)S(1)} all-gather(bf16[1,1,1536]{2,1,0:T(2,128)(2,1)S(1)} %reshape.259), channel_id=2, replica_groups=mesh['dp'=8,'ctx'=4] {'dp'}, dimensions={0}, use_global_device_ids=true | all-gather | bytes 27648 | tf_op jit(solution)/shard_map/all_gather | solution.py:117
  53.4 27.0 %all_gather.40 = bf16[256,1024]{1,0:T(8,128)(2,1)S(1)} all-gather(bf16[256,128]{1,0:T(8,128)(2,1)S(1)} %copy-done.6), channel_id=1, replica_groups=mesh['dp'=8,'ctx'=4] {'dp'}, dimensions={1}, use_global_device_ids=true | all-gather | bytes 589824 | tf_op jit(solution)/shard_map/all_gather | solution.py:142
  80.7 35.4 %all-gather.15.cloned.1.call-done = bf16[1024,3,256]{0,2,1:T(8,128)(2,1)} async-done(((bf16[128,3,256]{0,2,1:T(8,128)(2,1)}), bf16[1024,3,256]{0,2,1:T(8,128)(2,1)}) %all-gather.15.cloned.1.call-update) | async-done | bytes 1572880 | tf_op jit(solution)/shard_map/all_gather | solution.py:141
  125.8 22.5 %reduce-scatter.13.cloned.1.call-done = bf16[128,1024]{1,0:T(8,128)(2,1)} async-done(((bf16[512,1024]{1,0:T(8,128)(2,1)}), bf16[128,1024]{1,0:T(8,128)(2,1)}) %reduce-scatter.13.cloned.1.call-update) | async-done | bytes 262160 | tf_op jit(solution)/shard_map/reduce_scatter | solution.py:175
  154.0 45.4 %all-gather.19.cloned.1.call-done = bf16[1024,1024]{1,0:T(8,128)(2,1)} async-done(((bf16[128,1024]{1,0:T(8,128)(2,1)}), bf16[1024,1024]{1,0:T(8,128)(2,1)}) %all-gather.19.cloned.1.call-update) | async-done | bytes 2097168 | tf_op jit(solution)/shard_map/all_gather | solution.py:143
  199.4 17.2 %all-gather.17.cloned.1.call-done = bf16[512,1024]{1,0:T(8,128)(2,1)} async-done(((bf16[128,1024]{1,0:T(8,128)(2,1)}), bf16[512,1024]{1,0:T(8,128)(2,1)}) %all-gather.17.cloned.1.call-update) | async-done | bytes 1048592 | tf_op jit(solution)/shard_map/all_gather | solution.py:185
  216.6 4.6 fusion.85
  221.2 13.6 %all-gather.25.cloned.1.call-done = bf16[1,512,1024]{2,1,0:T(8,128)(2,1)} async-done(((bf16[1,128,1024]{2,1,0:T(8,128)(2,1)}), bf16[1,512,1024]{2,1,0:T(8,128)(2,1)}) %all-gather.25.cloned.1.call-update) | async-done | bytes 1048592 | tf_op jit(solution)/shard_map/all_gather | solution.py:163
  234.8 52.4 %all-gather.21.cloned.1.call-done = bf16[1024,1024]{1,0:T(8,128)(2,1)} async-done(((bf16[1024,128]{1,0:T(8,128)(2,1)}), bf16[1024,1024]{1,0:T(8,128)(2,1)}) %all-gather.21.cloned.1.call-update) | async-done | bytes 2097168 | tf_op jit(solution)/shard_map/all_gather | solution.py:144
  287.2 5.1 fusion.83
  295.6 4.8 convolution_convert_fusion.5
  300.5 18.2 %reduce-scatter.17.cloned.1.call-done = bf16[128,1024]{1,0:T(8,128)(2,1)} async-done(((bf16[512,1024]{1,0:T(8,128)(2,1)}), bf16[128,1024]{1,0:T(8,128)(2,1)}) %reduce-scatter.17.cloned.1.call-update) | async-done | bytes 262160 | tf_op jit(solution)/shard_map/reduce_scatter | solution.py:204
  320.0 26.1 %reduce-scatter.15.cloned.1.call-done = bf16[128,1024]{1,0:T(8,128)(2,1)} async-done(((bf16[512,1024]{1,0:T(8,128)(2,1)}), bf16[128,1024]{1,0:T(8,128)(2,1)}) %reduce-scatter.15.cloned.1.call-update) | async-done | bytes 262160 | tf_op jit(solution)/shard_map/reduce_scatter | solution.py:191
  349.1 16.6 %all-gather.23.cloned.1.call-done = bf16[512,1024]{1,0:T(8,128)(2,1)} async-done(((bf16[128,1024]{1,0:T(8,128)(2,1)}), bf16[512,1024]{1,0:T(8,128)(2,1)}) %all-gather.23.cloned.1.call-update) | async-done | bytes 1048592 | tf_op jit(solution)/shard_map/all_gather | solution.py:215
  373.8 7.5 fusion.22
  381.3 9.0 %fusion.80 = (f32[4,64]{1,0:T(4,128)S(1)}, bf16[512,4,64]{0,2,1:T(8,128)(2,1)S(1)}) fusion(bf16[512,4,64]{0,2,1:T(8,128)(2,1)S(1)} %bitcast.205, f32[4,512,512]{1,2,0:T(8,128)} %fusion.86, f32[4,512]{1,0:T(4,128)S(1)} %log_add_fusion, f32[4,512,512]{1,2,0:T(8,128)} %copy-done.1, pred[512,512]{0,1:T(8,128)(4,1)S(1)} %fusion.29), kind=kOutput, calls=%fused_computation.145 | convolution fusion | flops 148113664 | bytes 9184256 | tf_op jit(solution)/shard_map/hqk,khd->qhd/dot_general | solution.py:71
  394.0 4.8 convolution_convert_fusion
  398.8 4.1 copy.75
  404.0 3.8 convolution_convert_fusion.1
  420.9 70.0 %reduce-scatter.27.cloned.1.call-done = bf16[128,1024]{1,0:T(8,128)(2,1)} async-done(((bf16[1024,1024]{1,0:T(8,128)(2,1)}), bf16[128,1024]{1,0:T(8,128)(2,1)}) %reduce-scatter.27.cloned.1.call-update) | async-done | bytes 262160
  492.9 69.0 %reduce-scatter.23.cloned.1.call-done = bf16[128,1024]{1,0:T(8,128)(2,1)} async-done(((bf16[1024,1024]{1,0:T(8,128)(2,1)}), bf16[128,1024]{1,0:T(8,128)(2,1)}) %reduce-scatter.23.cloned.1.call-update) | async-done | bytes 262160 | tf_op jit(solution)/shard_map/reduce_scatter | solution.py:243
  563.6 63.8 %reduce-scatter.25.cloned.1.call-done = bf16[128,256]{1,0:T(8,128)(2,1)} async-done(((bf16[1024,256]{1,0:T(8,128)(2,1)}), bf16[128,256]{1,0:T(8,128)(2,1)}) %reduce-scatter.25.cloned.1.call-update) | async-done | bytes 65552
  630.1 65.7 %reduce-scatter.21.cloned.1.call-done = bf16[128,3,256]{2,0,1:T(8,128)(2,1)} async-done(((bf16[1024,3,256]{2,0,1:T(8,128)(2,1)}), bf16[128,3,256]{2,0,1:T(8,128)(2,1)}) %reduce-scatter.21.cloned.1.call-update) | async-done | bytes 196624 | tf_op jit(solution)/shard_map/reduce_scatter | solution.py:241
  697.5 54.9 %all-gather.27.cloned.1.call-done = f32[256,1536]{1,0:T(8,128)} async-done(((f32[8,1536]{1,0:T(8,128)}), f32[256,1536]{1,0:T(8,128)}) %all-gather.27.cloned.1.call-update) | async-done | bytes 1572880 | tf_op jit(solution)/shard_map/all_gather | solution.py:264
  (150 shorter events, 73.4 us)
Async XLA Ops:
  7.2 46.3 %copy-start.6 = (bf16[256,128]{1,0:T(8,128)(2,1)S(1)}, bf16[256,128]{1,0:T(8,128)(2,1)}, u32[]{:S(2)}) copy-start(bf16[256,128]{1,0:T(8,128)(2,1)} %param.23) | copy-start | bytes 196612
  7.2 73.3 %copy-start.8 = (s32[1,512]{1,0:T(1,128)S(1)}, s32[1,512]{1,0:T(1,128)}, u32[]{:S(2)}) copy-start(s32[1,512]{1,0:T(1,128)} %param.17) | copy-start | bytes 6148
  7.2 73.5 %all-gather.13.cloned.1.call-start = ((), (), s32[]{:S(2)}) async-start(), calls=%async_computation.8 | async-start | bytes 1310720 | tf_op jit(solution)/shard_map/all_gather | solution.py:162
  51.4 64.8 %all-gather.15.cloned.1.call-start = ((), (), s32[]{:S(2)}) async-start(), calls=%async_computation.9 | async-start | bytes 1769472 | tf_op jit(solution)/shard_map/all_gather | solution.py:141
  53.2 95.1 %reduce-scatter.13.cloned.1.call-start = ((), (), s32[]{:S(2)}) async-start(), calls=%async_computation.10 | async-start | bytes 1310720 | tf_op jit(solution)/shard_map/reduce_scatter | solution.py:175
  123.7 24.6 %copy-start = (bf16[1,128,1024]{2,1,0:T(8,128)(2,1)S(1)}, bf16[1,128,1024]{2,1,0:T(8,128)(2,1)}, u32[]{:S(2)}) copy-start(bf16[1,128,1024]{2,1,0:T(8,128)(2,1)} %param.16) | copy-start | bytes 786436
  125.2 74.2 %all-gather.19.cloned.1.call-start = ((), (), s32[]{:S(2)}) async-start(), calls=%async_computation.12 | async-start | bytes 2359296 | tf_op jit(solution)/shard_map/all_gather | solution.py:143
  125.7 90.9 %all-gather.17.cloned.1.call-start = ((), (), s32[]{:S(2)}) async-start(), calls=%async_computation.11 | async-start | bytes 1310720 | tf_op jit(solution)/shard_map/all_gather | solution.py:185
  152.4 82.4 %all-gather.25.cloned.1.call-start = ((), (), s32[]{:S(2)}) async-start(), calls=%async_computation.20 | async-start | bytes 1310720 | tf_op jit(solution)/shard_map/all_gather | solution.py:163
  153.0 134.2 %all-gather.21.cloned.1.call-start = ((), (), s32[]{:S(2)}) async-start(), calls=%async_computation.13 | async-start | bytes 2359296 | tf_op jit(solution)/shard_map/all_gather | solution.py:144
  153.8 164.9 %reduce-scatter.17.cloned.1.call-start = ((), (), s32[]{:S(2)}) async-start(), calls=%async_computation.15 | async-start | bytes 1310720 | tf_op jit(solution)/shard_map/reduce_scatter | solution.py:204
  295.5 23.2 %copy-start.2 = (bf16[128,1024]{1,0:T(8,128)(2,1)S(1)}, bf16[128,1024]{1,0:T(8,128)(2,1)}, u32[]{:S(2)}) copy-start(bf16[128,1024]{1,0:T(8,128)(2,1)} %reduce-scatter.13.cloned.1.call-done) | copy-start | bytes 786436
  295.6 50.5 %copy-start.3 = (bf16[1,128,1024]{2,1,0:T(8,128)(2,1)S(1)}, bf16[1,128,1024]{2,1,0:T(8,128)(2,1)}, u32[]{:S(2)}) copy-start(bf16[1,128,1024]{2,1,0:T(8,128)(2,1)} %param.31) | copy-start | bytes 786436
  295.6 50.5 %reduce-scatter.15.cloned.1.call-start = ((), (), s32[]{:S(2)}) async-start(), calls=%async_computation.14 | async-start | bytes 1310720 | tf_op jit(solution)/shard_map/reduce_scatter | solution.py:191
  300.4 65.3 %all-gather.23.cloned.1.call-start = ((), (), s32[]{:S(2)}) async-start(), calls=%async_computation.16 | async-start | bytes 1310720 | tf_op jit(solution)/shard_map/all_gather | solution.py:215
  348.9 70.0 %reduce-scatter.19.cloned.1.call-start = ((), (), s32[]{:S(2)}) async-start(), calls=%async_computation.17 | async-start | bytes 1310720 | tf_op jit(solution)/shard_map/reduce_scatter | solution.py:230
  371.1 19.3 %copy-start.11 = (bf16[512,4,64]{0,2,1:T(8,128)(2,1)}, bf16[512,4,64]{0,2,1:T(8,128)(2,1)S(1)}, u32[]{:S(2)}) copy-start(bf16[512,4,64]{0,2,1:T(8,128)(2,1)S(1)} %get-tuple-element.29) | copy-start | bytes 786436
  381.3 9.1 %copy-start.12 = (bf16[4,64,512]{2,1,0:T(8,128)(2,1)}, bf16[4,64,512]{2,1,0:T(8,128)(2,1)S(1)}, u32[]{:S(2)}) copy-start(bf16[4,64,512]{2,1,0:T(8,128)(2,1)S(1)} %fusion.22) | copy-start | bytes 786436
  393.9 97.0 %reduce-scatter.27.cloned.1.call-start = ((), (), s32[]{:S(2)}) async-start(), calls=%async_computation.23 | async-start | bytes 2359296
  402.8 159.0 %reduce-scatter.23.cloned.1.call-start = ((), (), s32[]{:S(2)}) async-start(), calls=%async_computation.19 | async-start | bytes 2359296 | tf_op jit(solution)/shard_map/reduce_scatter | solution.py:243
  407.9 219.5 %reduce-scatter.25.cloned.1.call-start = ((), (), s32[]{:S(2)}) async-start(), calls=%async_computation.22 | async-start | bytes 589824
  410.5 285.3 %reduce-scatter.21.cloned.1.call-start = ((), (), s32[]{:S(2)}) async-start(), calls=%async_computation.18 | async-start | bytes 1769472 | tf_op jit(solution)/shard_map/reduce_scatter | solution.py:241
  414.9 337.4 %all-gather.27.cloned.1.call-start = ((), (), s32[]{:S(2)}) async-start(), calls=%async_computation.21 | async-start | bytes 1622016 | tf_op jit(solution)/shard_map/all_gather | solution.py:264
  418.9 210.1 %copy-start.5 = (bf16[128,1024]{1,0:T(8,128)(2,1)S(1)}, bf16[128,1024]{1,0:T(8,128)(2,1)}, u32[]{:S(2)}) copy-start(bf16[128,1024]{1,0:T(8,128)(2,1)} %reduce-scatter.19.cloned.1.call-done) | copy-start | bytes 786436
  (7 other events, 15.5 us)
Sparse Core Ops, SparseCore 0:
  51.5 17.5 all-gather.12
  71.7 44.3 all-gather.14
  125.3 22.9 reduce-scatter.12
  150.3 49.0 all-gather.18
  201.4 15.2 all-gather.16
  218.0 16.6 all-gather.24
  236.8 50.3 all-gather.20
  295.7 22.9 reduce-scatter.16
  321.2 24.7 reduce-scatter.14
  349.0 16.6 all-gather.22
  394.0 24.7 reduce-scatter.18
  422.3 68.6 reduce-scatter.26
  494.4 67.3 reduce-scatter.22
  565.6 61.7 reduce-scatter.24
  630.7 65.0 reduce-scatter.20
  698.6 53.7 all-gather.26
